TPU v7x, 32 devices: a whole 2x2x4 slice. The times are simulated.
32 devices in a mesh: arc: 16 (over z, x, core), ord: 2 (over y).
Axes of the slice: x: 2, y: 2, z: 4, core: 2. Of those that a mesh axis runs over, the one named last changes fastest.
Arguments:
- design: bfloat16 [16384, 32768], P('arc', 'ord'), may hold values from -4 to 4
- arc_lengths: int32 [16], P('arc'), may hold values from 1 to 1024, 10240 in all
- kaula_prior: float32 [1024], replicated, may hold values from 1 to 20
Outputs:
- factor: float32 [1024, 32768], P('arc', 'ord')
Inputs may be any that keep to these rules, and one draw needn't show every extreme that they name: `arc_lengths`: some arc has all 1024 slots live.
All inputs are finite; a program needn't handle non-finite values. No bound on the sum of `arc_lengths` on one device may be relied on, other than what follows from the above.
Results may differ from a plain program's by a relative error of at most 0.0003.
Values may be sent and summed in bfloat16 or wider, within the bound.
A program may use at most 320 MiB of HBM per device.

v0:
```python
import math

import jax
import jax.numpy as jnp
from jax import lax
from jax.sharding import PartitionSpec as P

TILE = 512
PANELS = 2


def broadcast(block, axis, source):
    block = jnp.where(lax.axis_index(axis) == source, block, jnp.zeros_like(block))
    return lax.psum(block, axis)


def apply_panels(matrix, lowers, couplings):
    blocks = [matrix[p * TILE : (p + 1) * TILE] for p in range(PANELS)]
    for p in range(PANELS):
        blocks[p] = jax.scipy.linalg.solve_triangular(lowers[p], blocks[p], lower=True)
        for q in range(p + 1, PANELS):
            blocks[q] = blocks[q] - jnp.dot(
                couplings[p, q].T, blocks[p], precision=lax.Precision.HIGHEST
            )
    return jnp.concatenate(blocks, axis=0)


def on_device(design, arc_lengths, kaula_prior):
    obs_dev, ord_cols = design.shape
    arcs_here = arc_lengths.shape[0]
    arc_steps = obs_dev // arcs_here
    row_block = min(256, arc_steps)
    slab_rows = TILE * PANELS
    pieces = []
    for panel_index in range(PANELS):
        owner = panel_index * TILE // ord_cols
        offset = panel_index * TILE % ord_cols
        piece = design[:, offset : offset + TILE]
        pieces.append(broadcast(piece, "ord", owner))
    slab_cols = jnp.concatenate(pieces, axis=1)
    position = lax.broadcasted_iota(jnp.int32, (row_block, 1), 0)
    partial_value = jnp.zeros((slab_rows, ord_cols), jnp.float32)
    gram_part = jnp.zeros((slab_rows, slab_rows), jnp.float32)
    arc_slot = 0
    length = arc_lengths[arc_slot]
    blocks_live = (length + row_block - 1) // row_block

    def accumulate(step_idx, running, arc_slot=arc_slot, length=length):
        first_row = arc_slot * arc_steps + step_idx * row_block
        slab_block = lax.dynamic_slice_in_dim(slab_cols, first_row, row_block, 0)
        tile_block = lax.dynamic_slice_in_dim(design, first_row, row_block, 0)
        is_live = position + step_idx * row_block < length
        live_block = jnp.where(is_live, slab_block, jnp.zeros((), slab_block.dtype))
        dims = (((0,), (0,)), ((), ()))
        normal_acc = running[0] + lax.dot_general(
            live_block, tile_block, dims, preferred_element_type=jnp.float32
        )
        gram_acc = running[1] + lax.dot_general(
            live_block, slab_block, dims, preferred_element_type=jnp.float32
        )
        return (normal_acc, gram_acc)

    partial_value, gram_part = lax.fori_loop(0, blocks_live, accumulate, (partial_value, gram_part))
    inverse_norm = 1.0 / math.sqrt(lax.axis_size("arc") * obs_dev)
    square_ids = lax.broadcasted_iota(jnp.int32, (slab_rows, slab_rows), 0)
    square_cols = lax.broadcasted_iota(jnp.int32, (slab_rows, slab_rows), 1)
    gram = lax.psum(gram_part, "arc") * inverse_norm
    gram = gram + jnp.where(square_ids == square_cols, kaula_prior[:, None], 0.0)
    gram_blocks = [gram[p * TILE : (p + 1) * TILE] for p in range(PANELS)]
    lowers = []
    couplings = {}
    for p in range(PANELS):
        lower_factor = jnp.linalg.cholesky(gram_blocks[p][:, p * TILE : (p + 1) * TILE])
        lowers.append(lower_factor)
        gram_blocks[p] = jax.scipy.linalg.solve_triangular(lower_factor, gram_blocks[p], lower=True)
        for q in range(p + 1, PANELS):
            upper_tile = gram_blocks[p][:, q * TILE : (q + 1) * TILE]
            couplings[p, q] = upper_tile
            gram_blocks[q] = gram_blocks[q] - jnp.dot(
                upper_tile.T, gram_blocks[p], precision=lax.Precision.HIGHEST
            )
    row_index = lax.broadcasted_iota(jnp.int32, (slab_rows, 1), 0)
    summed = lax.psum_scatter(partial_value, "arc", scatter_dimension=1, tiled=True) * inverse_norm
    width = ord_cols // lax.axis_size("arc")
    col_first = lax.axis_index("ord") * ord_cols + lax.axis_index("arc") * width
    global_col = col_first + lax.broadcasted_iota(jnp.int32, (1, width), 1)
    matrix = summed + jnp.where(row_index == global_col, kaula_prior[:, None], 0.0)
    share = apply_panels(matrix, lowers, couplings)
    factor = lax.all_to_all(share, "arc", split_axis=0, concat_axis=1, tiled=True)
    return factor


def solution(mesh):
    in_specs = (P("arc", "ord"), P("arc"), P())
    out_specs = P("arc", "ord")
    return jax.shard_map(
        on_device, mesh=mesh, in_specs=in_specs, out_specs=out_specs, check_vma=False
    )
```

profile of v0, /device:TPU:1, one launch (start us, length us, event | category | flops | bytes accessed | tf_op | source)
XLA Modules:
  0.0 1505.2 jit_solution(2302760153561612100)
XLA Ops:
  6.5 3.0 slice_select_fusion.1
  10.3 64.6 %all-reduce.7.cloned.1.call-done = (bf16[1024,512]{1,0:T(8,128)(2,1)}, bf16[1024,512]{1,0:T(8,128)(2,1)}) async-done(((bf16[1024,512]{1,0:T(8,128)(2,1)}, bf16[1024,512]{1,0:T(8,128)(2,1)}), (bf16[1024,512]{1,0:T(8,128)(2,1)}, bf16[1024,512]{1,0:T(8,128)(2,1)})) %all-reduce.7.cloned.1.call-update) | async-done | bytes 2097168 | tf_op jit(solution)/shard_map/psum | solution.py:14
  74.9 1.8 pad_maximum_fusion
  76.7 21.0 %broadcast_in_dim.35 = f32[1024,16384]{1,0:T(8,128)} broadcast(f32[]{:T(128)} %constant.143.clone.1), dimensions={} | broadcast | bytes 67108864 | tf_op jit(solution)/shard_map/broadcast_in_dim | solution.py:42
  97.7 2.5 broadcast_in_dim.36.clone
  100.3 153.3 %while.19 = (s32[]{:T(128)}, f32[1024,16384]{1,0:T(8,128)}, f32[1024,1024]{1,0:T(8,128)}, s32[]{:T(128)}, s32[]{:T(128)}, /*index=5*/bf16[1024,1024]{1,0:T(8,128...) while((s32[]{:T(128)}, f32[1024,16384]{1,0:T(8,128)}, ...), condition=%wide.region_3.4_spmd.clone, body=%wide.region_2.3_spmd.clone.sunk | while | flops 9145156608 | bytes 152571312 | solution.py:63
  101.0 45.4 %convolution_add_fusion.4 = f32[1024,16384]{1,0:T(8,128)} fusion(f32[1024,16384]{1,0:T(8,128)} %get-tuple-element.287, bf16[1024,16384]{1,0:T(8,128)(2,1)} %get-tuple-element.303, s32[]{:T(128)S(6)} %select_n.66, pred[256]{0:T(512)(128)(4,1)S(1)} %compare_reduce_fusion.10, bf16[1024,1024]{1,0:T(8,128)(2,1)S(1)} %get-tuple-element.302), kind=kOutput, calls=%fused_computation.5.clone.3 | convolution fusion | flops 8606973952 | bytes 143132160 | tf_op jit(solution)/shard_map/while/body/dot_general | solution.py:55
  146.4 5.0 convolution_add_fusion.5
  152.1 45.4 %convolution_add_fusion.4 = f32[1024,16384]{1,0:T(8,128)} fusion(f32[1024,16384]{1,0:T(8,128)} %get-tuple-element.287, bf16[1024,16384]{1,0:T(8,128)(2,1)} %get-tuple-element.303, s32[]{:T(128)S(6)} %select_n.66, pred[256]{0:T(512)(128)(4,1)S(1)} %compare_reduce_fusion.10, bf16[1024,1024]{1,0:T(8,128)(2,1)S(1)} %get-tuple-element.302), kind=kOutput, calls=%fused_computation.5.clone.3 | convolution fusion | flops 8606973952 | bytes 143132160 | tf_op jit(solution)/shard_map/while/body/dot_general | solution.py:55
  197.5 5.0 convolution_add_fusion.5
  203.2 45.4 %convolution_add_fusion.4 = f32[1024,16384]{1,0:T(8,128)} fusion(f32[1024,16384]{1,0:T(8,128)} %get-tuple-element.287, bf16[1024,16384]{1,0:T(8,128)(2,1)} %get-tuple-element.303, s32[]{:T(128)S(6)} %select_n.66, pred[256]{0:T(512)(128)(4,1)S(1)} %compare_reduce_fusion.10, bf16[1024,1024]{1,0:T(8,128)(2,1)S(1)} %get-tuple-element.302), kind=kOutput, calls=%fused_computation.5.clone.3 | convolution fusion | flops 8606973952 | bytes 143132160 | tf_op jit(solution)/shard_map/while/body/dot_general | solution.py:55
  248.6 5.0 convolution_add_fusion.5
  253.6 5.3 copy.13
  259.0 65.9 %copy.15 = f32[1024,16384]{0,1:T(8,128)} copy(f32[1024,16384]{1,0:T(8,128)} %get-tuple-element.52) | data formatting | bytes 134217728 | tf_op jit(solution)/shard_map/while | solution.py:63
  325.0 95.0 %all-reduce.5.cloned.1.call-done = f32[1024,1024]{0,1:T(8,128)} async-done(((f32[1024,1024]{0,1:T(8,128)}), f32[1024,1024]{0,1:T(8,128)}) %all-reduce.5.cloned.1.call-update) | async-done | bytes 4194320 | tf_op jit(solution)/shard_map/psum | solution.py:67
  420.0 641.4 %reduce-scatter.2.cloned.1.call-done = f32[1024,1024]{0,1:T(8,128)} async-done(((f32[1024,16384]{0,1:T(8,128)}), f32[1024,1024]{0,1:T(8,128)}) %reduce-scatter.2.cloned.1.call-update) | async-done | bytes 4194320 | tf_op jit(solution)/shard_map/reduce_scatter | solution.py:83
  1061.4 5.5 select_add_fusion.1
  1067.0 1.8 copy-done
  1068.8 1.6 slice.141
  1070.7 1.4 fusion.70
  1072.2 11.7 cholesky.286
  1084.1 9.8 custom-call.28
  1094.5 11.7 cholesky.305
  1106.3 10.3 custom-call.29
  1117.2 11.7 cholesky.326
  1129.6 9.8 custom-call.30
  1140.0 11.7 cholesky.343
  1156.0 7.8 while.20
  1156.6 1.3 bitcast_dynamic-update-slice_fusion.4
  1158.5 1.3 bitcast_dynamic-update-slice_fusion.4
  1160.5 1.3 bitcast_dynamic-update-slice_fusion.4
  1162.4 1.3 bitcast_dynamic-update-slice_fusion.4
  1163.7 39.3 %custom-call.31 = f32[4,128,128]{1,2,0:T(8,128)S(1)} custom-call(f32[4,128,128]{2,1,0:T(8,128)S(1)} %get-tuple-element.90), custom_call_target="InvertDiagBlocksLowerTriangular" | custom-call | tf_op jit(solution)/shard_map/jit(_solve_triangular)/triangular_solve | solution.py:20
  1203.1 1.7 fusion.73
  1204.7 2.0 convolution_subtract_fusion.4
  1207.4 2.9 convolution_subtract_fusion.1
  1210.9 3.8 fusion.54
  1215.4 3.5 fusion.23
  1219.2 1.3 copy.17
  1220.5 1.8 fusion.69
  1223.3 11.7 cholesky.358
  1235.2 9.8 custom-call.33
  1248.2 11.7 cholesky.377
  1261.3 10.0 custom-call.34
  1274.4 13.2 cholesky.398
  1287.5 1.5 select_reduce_fusion.1
  1289.7 11.3 custom-call.35
  1303.2 11.7 cholesky.415
  1319.3 11.7 while.21
  1320.0 2.3 bitcast_dynamic-update-slice_fusion.5
  1322.9 2.3 bitcast_dynamic-update-slice_fusion.5
  1325.9 2.3 bitcast_dynamic-update-slice_fusion.5
  1328.8 2.2 bitcast_dynamic-update-slice_fusion.5
  1331.0 40.1 %custom-call.36 = f32[4,128,128]{1,2,0:T(8,128)} custom-call(f32[4,128,128]{2,1,0:T(8,128)S(1)} %get-tuple-element.92), custom_call_target="InvertDiagBlocksLowerTriangular" | custom-call | tf_op jit(solution)/shard_map/jit(_solve_triangular)/triangular_solve | solution.py:20
  1371.1 1.8 fusion.75
  1373.0 2.1 convolution_subtract_fusion.5
  1375.7 3.0 convolution_subtract_fusion.2
  1379.3 3.7 fusion.57
  1383.7 3.6 slice_subtract_fusion
  1388.2 1.8 convolution_subtract_fusion.3
  1390.7 2.7 convolution_subtract_fusion
  1394.1 3.7 fusion.51
  1399.1 96.8 %all_to_all.19 = f32[16,64,1024]{2,1,0:T(8,128)S(1)} all-to-all(f32[16,64,1024]{2,1,0:T(8,128)S(1)} %bitcast.117), channel_id=1, replica_groups=mesh['arc'=16,'ord'=2] {'arc'}, dimensions={0} | all-to-all | bytes 8388608 | tf_op jit(solution)/shard_map/all_to_all | solution.py:89
  1495.9 2.3 copy.32
  (95 shorter events, 33.3 us)
Async XLA Ops:
  6.5 68.4 %all-reduce.7.cloned.1.call-start = ((), (), s32[]{:S(2)}) async-start(), calls=%async_computation.4 | async-start | bytes 4194304 | tf_op jit(solution)/shard_map/psum | solution.py:14
  9.6 410.4 %all-reduce.5.cloned.1.call-start = ((), (), s32[]{:S(2)}) async-start(), calls=%async_computation.2 | async-start | bytes 8388608 | tf_op jit(solution)/shard_map/psum | solution.py:67
  259.0 802.4 %reduce-scatter.2.cloned.1.call-start = ((), (), s32[]{:S(2)}) async-start(), calls=%async_computation.3 | async-start | bytes 71303168 | tf_op jit(solution)/shard_map/reduce_scatter | solution.py:83
  324.9 736.4 %copy-start.7 = (f32[1024]{0:T(1024)S(1)}, f32[1024]{0:T(1024)}, u32[]{:S(2)}) copy-start(f32[1024]{0:T(1024)} %param.10) | copy-start | bytes 12292
  1066.9 1.9 copy-start
  1163.7 43.7 %copy-start.3 = (f32[512,512]{1,0:T(8,128)}, f32[512,512]{1,0:T(8,128)S(1)}, u32[]{:S(2)}) copy-start(f32[512,512]{1,0:T(8,128)S(1)} %get-tuple-element.346) | copy-start | bytes 3145732
  1214.8 4.2 copy-start.2
  1222.3 1.0 copy-start.4
  1247.5 0.7 copy-start.5
  1371.1 8.2 copy-start.1
  1383.7 3.6 copy-start.6
Sparse Core Ops, SparseCore 0:
  9.7 65.1 all-reduce.6
  259.1 160.8 all-reduce.4
  424.2 637.1 reduce-scatter.1
where the time goes:
time: 1510 us
  waiting for transfers between devices  801 us (53%)
  other arithmetic  260 us (17%)
  matrix products  203 us (13%)
  local copies, waits for them, and re-layouts  124 us (8%)
  blocking collectives  96.8 us (6%)
  between operations  19.8 us (1%)
    reduce_scatter x1, waiting for transfers between devices, on_device(): lax.psum_scatter(partial_value, 'arc', scatter_dimension=1, tiled=True)  641 us
    another operation x29, other arithmetic, on_device(): jnp.linalg.cholesky(gram_blocks[p][:, p * TILE:(p + 1) * TILE])  163 us
    dot_general x3, matrix products, accumulate(): lax.dot_general(live_block, tile_block, dims, preferred_element_type=jnp....  136 us
    all_to_all x1, blocking collectives, on_device(): lax.all_to_all(share, 'arc', split_axis=0, concat_axis=1, tiled=True)  96.8 us
    psum x1, waiting for transfers between devices, on_device(): gram = lax.psum(gram_part, 'arc') * inverse_norm  95 us
    another operation x5, other arithmetic, apply_panels(): jax.scipy.linalg.solve_triangular(lowers[p], blocks[p], lower=True)  80.7 us
    while x2, local copies, waits for them, and re-layouts, on_device(): lax.fori_loop(0, blocks_live, accumulate, (partial_value, gram_part))  71.3 us
    psum x1, waiting for transfers between devices, broadcast(): return lax.psum(block, axis)  64.6 us
  transfers between devices with their start and end apart: 3, of which 3 were waited for; matrix products, arithmetic and copies ran while one was open for 4% of the time, Pallas kernels for 0%

commit v1 on v0

--- a/solution.py
+++ b/solution.py
@@ -3,6 +3,8 @@
 import jax
 import jax.numpy as jnp
 from jax import lax
+from jax.experimental import pallas as pl
+from jax.experimental.pallas import tpu as pltpu
 from jax.sharding import PartitionSpec as P
 
 TILE = 512
@@ -90,9 +92,170 @@
     return factor
 
 
+NB = 128
+GROUP = 128
+LEVELS = 32767.0
+
+
+def diagonal_inverse(block):
+    tiles = NB // 8
+    sub = lax.broadcasted_iota(jnp.int32, (8, NB), 0)
+    lane = lax.broadcasted_iota(jnp.int32, (8, NB), 1)
+    rest = [block[8 * t : 8 * t + 8] for t in range(tiles)]
+    inv = [jnp.where(sub + 8 * t == lane, 1.0, 0.0).astype(jnp.float32) for t in range(tiles)]
+    for j in range(NB):
+        t, s = j // 8, j % 8
+        column = [jnp.broadcast_to(rest[i][:, j : j + 1], (8, NB)) for i in range(t, tiles)]
+        recip = 1.0 / jnp.broadcast_to(column[0][s : s + 1], (8, NB))
+        row = jnp.broadcast_to(rest[t][s : s + 1], (8, NB)) * recip
+        inv_row = jnp.broadcast_to(inv[t][s : s + 1], (8, NB)) * recip
+        for i in range(t, tiles):
+            c = column[i - t]
+            if i == t:
+                c = jnp.where(sub > s, c, 0.0)
+            rest[i] = rest[i] - c * row
+            inv[i] = inv[i] - c * inv_row
+    for t in range(tiles):
+        pivot = jnp.sum(jnp.where(sub + 8 * t == lane, rest[t], 0.0), axis=1, keepdims=True)
+        inv[t] = inv[t] * (1.0 / jnp.sqrt(pivot))
+    return jnp.concatenate(inv, axis=0)
+
+
+def cholesky_inverse_kernel(gram_ref, out_ref, work, left, right):
+    size = gram_ref.shape[0]
+    blocks = size // NB
+    work[...] = gram_ref[...]
+    rows = lax.broadcasted_iota(jnp.int32, (NB, size), 0)
+    cols = lax.broadcasted_iota(jnp.int32, (NB, size), 1)
+    for i in range(blocks):
+        out_ref[i * NB : (i + 1) * NB, :] = jnp.where(rows + i * NB == cols, 1.0, 0.0)
+
+    def step(k, carry):
+        first = pl.multiple_of(k * NB, NB)
+        here = pl.ds(first, NB)
+        inverse = diagonal_inverse(work[here, here])
+        left[...] = jnp.dot(inverse, work[here, :], precision=lax.Precision.HIGHEST)
+        right[...] = jnp.dot(inverse, out_ref[here, :], precision=lax.Precision.HIGHEST)
+        out_ref[here, :] = right[...]
+
+        def update(i, carry):
+            there = pl.ds(pl.multiple_of(i * NB, NB), NB)
+            lower = left[:, there].T
+            work[there, :] -= jnp.dot(lower, left[...], precision=lax.Precision.HIGHEST)
+            out_ref[there, :] -= jnp.dot(lower, right[...], precision=lax.Precision.HIGHEST)
+            return carry
+
+        return lax.fori_loop(k + 1, blocks, update, carry)
+
+    lax.fori_loop(0, blocks, step, 0)
+
+
+def cholesky_inverse(gram):
+    size = gram.shape[0]
+    return pl.pallas_call(
+        cholesky_inverse_kernel,
+        out_shape=jax.ShapeDtypeStruct((size, size), jnp.float32),
+        in_specs=[pl.BlockSpec(memory_space=pltpu.VMEM)],
+        out_specs=pl.BlockSpec(memory_space=pltpu.VMEM),
+        scratch_shapes=[
+            pltpu.VMEM((size, size), jnp.float32),
+            pltpu.VMEM((NB, size), jnp.float32),
+            pltpu.VMEM((NB, size), jnp.float32),
+        ],
+        compiler_params=pltpu.CompilerParams(vmem_limit_bytes=24 << 20),
+        cost_estimate=pl.CostEstimate(
+            flops=100_000_000_000, bytes_accessed=2 * size * size * 4, transcendentals=0
+        ),
+    )(gram)
+
+
+def quantize(value, group):
+    height, width = value.shape
+    grouped = value.reshape(height // group, group, width)
+    top = jnp.max(jnp.abs(grouped), axis=1, keepdims=True)
+    factor = jnp.where(top > 1e-30, LEVELS / jnp.maximum(top, 1e-30), 0.0)
+    code = jnp.round(grouped * factor).astype(jnp.int16).reshape(height, width)
+    return code, top.reshape(height // group, width) * (1.0 / LEVELS)
+
+
+def dequantize(code, scale, group):
+    height, width = code.shape
+    grouped = code.astype(jnp.float32).reshape(height // group, group, width)
+    return (grouped * scale[:, None, :]).reshape(height, width)
+
+
+def send(value, bit):
+    size = lax.axis_size("arc")
+    return lax.ppermute(value, "arc", [(i, i ^ bit) for i in range(size)])
+
+
+def send_coded(value, bit):
+    code, scale = quantize(value, GROUP)
+    return dequantize(send(code, bit), send(scale, bit), GROUP)
+
+
+def on_device_paired(design, arc_lengths, kaula_prior):
+    obs_dev, ord_cols = design.shape
+    arcs = lax.axis_size("arc")
+    slab_rows = TILE * PANELS
+    width = ord_cols // arcs
+    me = lax.axis_index("arc")
+    core, x, z = me % 2, (me // 2) % 2, me // 4
+    inverse_norm = 1.0 / math.sqrt(arcs * obs_dev)
+    dims = (((0,), (0,)), ((), ()))
+
+    def product(a, b):
+        return lax.dot_general(a, b, dims, preferred_element_type=jnp.float32)
+
+    slab = design[:, :slab_rows]
+    arrived = lax.ppermute(slab, "ord", [(0, 1)])
+    slab = jnp.where(lax.axis_index("ord") == 0, slab, arrived)
+    position = lax.broadcasted_iota(jnp.int32, (obs_dev, 1), 0)
+    masked = jnp.where(position < arc_lengths[0], slab, jnp.zeros((), slab.dtype))
+
+    def pair(k, c):
+        parts = []
+        for flip in range(2):
+            block = ((z ^ k) * 2 + (x ^ flip)) * 2 + c
+            parts.append(lax.dynamic_slice(design, (0, block * width), (obs_dev, width)))
+        return jnp.concatenate(parts, axis=1)
+
+    others = {k: send(pair(k, 1 - core), 1) for k in (3, 2, 1, 0)}
+    masked_other = send(masked, 1)
+
+    gram = lax.psum_scatter(product(masked, slab), "arc", scatter_dimension=0, tiled=True)
+    gram = lax.all_gather(gram, "arc", axis=0, tiled=True) * inverse_norm
+    row_ids = lax.broadcasted_iota(jnp.int32, (slab_rows, slab_rows), 0)
+    col_ids = lax.broadcasted_iota(jnp.int32, (slab_rows, slab_rows), 1)
+    gram = gram + jnp.where(row_ids == col_ids, kaula_prior[:, None], 0.0)
+    inverse = cholesky_inverse(gram)
+
+    sums = {}
+    for k in (3, 2, 1, 0):
+        part = product(masked, pair(k, core)) + product(masked_other, others[k])
+        sums[k] = part[:, :width] + send_coded(part[:, width:], 2)
+        if k == 3:
+            from_three = send_coded(sums[3], 4)
+        if k == 2:
+            from_two = send_coded(sums[2] + from_three, 8)
+        if k == 1:
+            from_one = send_coded(sums[1], 4)
+    matrix = (sums[0] + from_one + from_two) * inverse_norm
+    holds_gram = (lax.axis_index("ord") == 0) & (me == 0)
+    matrix = jnp.where(holds_gram, gram, matrix)
+    share = jnp.dot(inverse, matrix, precision=lax.Precision.HIGHEST)
+    group = slab_rows // arcs
+    code, scale = quantize(share, group)
+    code = lax.all_to_all(code, "arc", split_axis=0, concat_axis=1, tiled=True)
+    scale = lax.all_to_all(scale, "arc", split_axis=0, concat_axis=1, tiled=True)
+    return code.astype(jnp.float32) * scale
+
+
 def solution(mesh):
     in_specs = (P("arc", "ord"), P("arc"), P())
     out_specs = P("arc", "ord")
+    paired = mesh.shape["arc"] == 16 and mesh.shape["ord"] == 2
     return jax.shard_map(
-        on_device, mesh=mesh, in_specs=in_specs, out_specs=out_specs, check_vma=False
+        on_device_paired if paired else on_device,
+        mesh=mesh, in_specs=in_specs, out_specs=out_specs, check_vma=False
     )

time: 1510 us -> 719 us (0.48)
  waiting for transfers between devices: 801 us -> 293 us
  Pallas kernels: 0 us -> 175 us
  other arithmetic: 260 us -> 97.1 us
  matrix products: 203 us -> 82 us
  local copies, waits for them, and re-layouts: 124 us -> 11.4 us
  blocking collectives: 96.8 us -> 0 us
  starting transfers between devices: 0.08 us -> 38.3 us
    reduce_scatter x1, waiting for transfers between devices: 641 us -> 39.4 us  [on_device_paired(): lax.psum_scatter(product(masked, slab), 'arc', scatter_dimension=0, tiled...]
    another operation x34 -> x0, other arithmetic: 243 us -> none  [the longest x29 163 us: on_device(): jnp.linalg.cholesky(gram_blocks[p][:, p * TILE:(p + 1) * TILE])]
    ppermute x0 -> x20, waiting for transfers between devices: none -> 209 us  [the longest x19 170 us: send(): return lax.ppermute(value, 'arc', [(i, i ^ bit) for i in range(size)])]
    pallas_call x0 -> x1, Pallas kernels: none -> 175 us  [cholesky_inverse(): pl.pallas_call(cholesky_inverse_kernel, out_shape=jax.ShapeDtypeStruct((s...]
    psum x2 -> x0, waiting for transfers between devices: 160 us -> none  [the longest x1 95 us: on_device(): gram = lax.psum(gram_part, 'arc') * inverse_norm]
    all_to_all x1 -> x0, blocking collectives: 96.8 us -> none  [on_device(): lax.all_to_all(share, 'arc', split_axis=0, concat_axis=1, tiled=True)]
    dot_general x8 -> x10, matrix products: 158 us -> 82 us  [the longest x9 63.2 us: product(): return lax.dot_general(a, b, dims, preferred_element_type=jnp.float32)]
    while x2 -> x0, local copies, waits for them, and re-layouts: 71.3 us -> none  [on_device(): lax.fori_loop(0, blocks_live, accumulate, (partial_value, gram_part))]
  transfers between devices with their start and end apart: 3 -> 24, of which waited for: 3 -> 8; matrix products, arithmetic and copies ran while one was open for 4% -> 22% of each run, Pallas kernels for 0% -> 0%
where the time goes in v1:
time: 719 us; the launch traced here: 711 us
  waiting for transfers between devices  293 us (41%)
  Pallas kernels  175 us (24%)
  other arithmetic  97.1 us (14%)
  matrix products  82 us (11%)
  starting transfers between devices  38.3 us (5%)
  between operations  14.7 us (2%)
  local copies, waits for them, and re-layouts  11.4 us (2%)
    pallas_call x1, Pallas kernels, cholesky_inverse(): pl.pallas_call(cholesky_inverse_kernel, out_shape=jax.ShapeDtypeStruct((s...  175 us
    ppermute x19, waiting for transfers between devices, send(): return lax.ppermute(value, 'arc', [(i, i ^ bit) for i in range(size)])  170 us
    dot_general x9, matrix products, product(): return lax.dot_general(a, b, dims, preferred_element_type=jnp.float32)  63.2 us
    all_to_all x1, waiting for transfers between devices, on_device_paired(): code = lax.all_to_all(code, 'arc', split_axis=0, concat_axis=1, tiled=True)  40.8 us
    reduce_scatter x1, waiting for transfers between devices, on_device_paired(): lax.psum_scatter(product(masked, slab), 'arc', scatter_dimension=0, tiled...  39.4 us
    ppermute x1, waiting for transfers between devices, on_device_paired(): arrived = lax.ppermute(slab, 'ord', [(0, 1)])  38.8 us
    convert_element_type x8, other arithmetic, quantize(): code = jnp.round(grouped * factor).astype(jnp.int16).reshape(height, width)  26.7 us
    dynamic_slice x1, other arithmetic, pair(): lax.dynamic_slice(design, (0, block * width), (obs_dev, width))  20.5 us
  transfers between devices with their start and end apart: 24, of which 8 were waited for; matrix products, arithmetic and copies ran while one was open for 22% of the time, Pallas kernels for 0%

profile of v1, /device:TPU:1, one launch (start us, length us, event | category | flops | bytes accessed | tf_op | source)
XLA Modules:
  0.0 711.1 jit_solution(18173518466794820395)
XLA Ops:
  6.5 3.8 constant_dynamic-slice_fusion.1
  10.3 5.3 collective-permute-start
  15.7 2.4 pad_maximum_fusion.3
  18.1 1.0 collective-permute-start.13
  19.8 38.8 %collective-permute-done = bf16[1024,1024]{1,0:T(8,128)(2,1)} collective-permute-done((bf16[1024,1024]{1,0:T(8,128)(2,1)S(1)}, bf16[1024,1024]{1,0:T(8,128)(2,1)}, u32[]{:S(2)}, u32[]{:S(2)}) %collective-permute-start) | collective-permute-done | bytes 2097184 | tf_op jit(solution)/shard_map/ppermute | solution.py:211
  58.6 20.5 %constant_dynamic-slice_fusion.15 = (bf16[1024,1024]{1,0:T(8,128)(2,1)}, bf16[1024,1024]{1,0:T(8,128)(2,1)S(1)}, bf16[1024,1024]{1,0:T(8,128)(2,1)}, bf16[1024,1...) fusion(bf16[1024,16384]{1,0:T(8,128)(2,1)} %param.3, ...), kind=kLoop, calls=%fused_computation.120 | loop fusion | flops 2097152 | bytes 65012792 | tf_op jit(solution)/shard_map/dynamic_slice | solution.py:220
  79.1 1.6 collective-permute-start.1
  80.8 4.9 pad_maximum_fusion
  85.7 2.5 pad_maximum_fusion.1
  88.7 2.4 pad_maximum_fusion.2
  91.2 6.0 fusion.56
  97.7 7.2 %fusion.66 = f32[1024,2048]{1,0:T(8,128)S(1)} fusion(bf16[1024,1024]{1,0:T(8,128)(2,1)} %collective-permute-done.1, bf16[1024,2048]{1,0:T(8,128)(2,1)} %collective-permute-done.13), kind=kOutput, calls=%fused_computation.131 | convolution fusion | flops 4294967296 | bytes 14680064 | tf_op jit(solution)/shard_map/dot_general | solution.py:208
  105.0 4.6 fusion.39
  109.6 0.5 bitcast_reduce_fusion.3
  110.1 2.5 fusion.30
  112.6 1.0 copy-done.1
  113.6 1.2 collective-permute-start.14
  115.0 7.6 %fusion.64 = f32[1024,2048]{1,0:T(8,128)S(1)} fusion(bf16[1024,1024]{1,0:T(8,128)(2,1)} %collective-permute-done.1, bf16[1024,2048]{1,0:T(8,128)(2,1)} %collective-permute-done.5), kind=kOutput, calls=%fused_computation.129 | convolution fusion | flops 4294967296 | bytes 14680064 | tf_op jit(solution)/shard_map/dot_general | solution.py:208
  122.7 4.6 fusion.45
  127.8 2.5 fusion.36
  130.3 0.9 copy-done
  131.2 1.3 collective-permute-start.6
  132.7 7.2 %fusion.65 = f32[1024,2048]{1,0:T(8,128)S(1)} fusion(bf16[1024,1024]{1,0:T(8,128)(2,1)} %collective-permute-done.1, bf16[1024,2048]{1,0:T(8,128)(2,1)} %collective-permute-done.10), kind=kOutput, calls=%fused_computation.130 | convolution fusion | flops 4294967296 | bytes 14680064 | tf_op jit(solution)/shard_map/dot_general | solution.py:208
  139.9 7.1 fusion.42
  147.0 39.4 %reduce-scatter.2.cloned.1.call-done = f32[64,1024]{1,0:T(8,128)} async-done(((f32[1024,1024]{1,0:T(8,128)}), f32[64,1024]{1,0:T(8,128)}) %reduce-scatter.2.cloned.1.call-update) | async-done | bytes 262160 | tf_op jit(solution)/shard_map/reduce_scatter | solution.py:226
  186.5 2.8 bitcast_reduce_fusion.4
  189.4 4.4 fusion.32
  194.0 4.0 bitcast_reduce_fusion.2
  198.0 4.3 fusion.28
  202.4 0.5 collective-permute-start.16
  202.9 11.0 %fusion.63 = f32[1024,2048]{1,0:T(8,128)} fusion(bf16[1024,1024]{1,0:T(8,128)(2,1)} %collective-permute-done.1, bf16[1024,2048]{1,0:T(8,128)(2,1)} %collective-permute-done.2), kind=kOutput, calls=%fused_computation.128 | convolution fusion | flops 4294967296 | bytes 14680064 | tf_op jit(solution)/shard_map/dot_general | solution.py:208
  213.8 8.0 %fusion.48 = f32[1024,2048]{1,0:T(8,128)S(1)} fusion(f32[1024,2048]{1,0:T(8,128)} %fusion.63, bf16[1024,1024]{1,0:T(8,128)(2,1)S(1)} %get-tuple-element.6, bf16[1024,1024]{1,0:T(8,128)(2,1)S(1)} %copy-done.5, bf16[1024,1024]{1,0:T(8,128)(2,1)S(1)} %copy-done.4), kind=kOutput, calls=%fused_computation.79 | convolution fusion | flops 4305453056 | bytes 23068672 | tf_op jit(solution)/shard_map/dot_general | solution.py:208
  222.5 0.7 fusion.38
  223.2 2.7 copy-done.2
  225.9 1.2 collective-permute-start.3
  227.1 0.6 collective-permute-start.12
  227.7 1.1 collective-permute-start.17
  228.7 3.0 bitcast_reduce_fusion.5
  231.7 4.4 fusion.34
  236.1 89.6 %collective-permute-done.12 = f32[8,1024]{1,0:T(8,128)S(1)} collective-permute-done((f32[8,1024]{1,0:T(8,128)S(1)}, f32[8,1024]{1,0:T(8,128)S(1)}, u32[]{:S(2)}, u32[]{:S(2)}) %collective-permute-start.12) | collective-permute-done | bytes 32800 | tf_op jit(solution)/shard_map/ppermute | solution.py:189
  325.6 1.2 collective-permute-start.8
  326.9 4.2 bitcast_reduce_fusion.1
  331.1 5.9 fusion.26
  337.0 2.4 collective-permute-start.18
  339.3 1.2 collective-permute-start.4
  340.7 1.8 collective-permute-done.4
  342.5 4.4 bitcast_multiply_fusion.13
  346.9 69.5 %collective-permute-done.9 = f32[8,1024]{1,0:T(8,128)S(1)} collective-permute-done((f32[8,1024]{1,0:T(8,128)S(1)}, f32[8,1024]{1,0:T(8,128)S(1)}, u32[]{:S(2)}, u32[]{:S(2)}) %collective-permute-start.9) | collective-permute-done | bytes 32800 | tf_op jit(solution)/shard_map/ppermute | solution.py:189
  416.4 4.3 bitcast_multiply_fusion.9
  420.7 9.5 %collective-permute-done.19 = f32[8,1024]{1,0:T(8,128)S(1)} collective-permute-done((f32[8,1024]{1,0:T(8,128)S(1)}, f32[8,1024]{1,0:T(8,128)S(1)}, u32[]{:S(2)}, u32[]{:S(2)}) %collective-permute-start.19) | collective-permute-done | bytes 32800 | tf_op jit(solution)/shard_map/ppermute | solution.py:189
  430.2 4.4 bitcast_multiply_fusion.1
  434.6 2.9 select_add_fusion.gram_ref
  437.5 175.1 %shard_map.37 = f32[1024,1024]{1,0:T(8,128)S(1)} custom-call(f32[1024,1024]{1,0:T(8,128)S(1)} %select_add_fusion.gram_ref), custom_call_target="tpu_custom_call" | custom-call | flops 99999997952 | bytes 8388608 | tf_op jit(solution)/shard_map/pallas_call | solution.py:155
  612.6 18.7 %bitcast_reduce_fusion = (f32[16,1024]{1,0:T(8,128)}, f32[1024,1024]{1,0:T(8,128)S(1)}) fusion(f32[1024,1024]{1,0:T(8,128)S(1)} %shard_map.37, f32[1024,1024]{1,0:T(8,128)S(1)} %select_add_fusion.gram_ref, f32[1024,1024]{1,0:T(8,128)} %bitcast_multiply_fusion.1, f32[1024,1024]{1,0:T(8,128)} %bitcast_multiply_fusion.9, ...), kind=kOutput, calls=%fused_computation.33 | convolution fusion | flops 12892225536 | bytes 29425664 | tf_op jit(solution)/shard_map/dot_general | solution.py:246
  631.4 0.9 broadcast_multiply_fusion.1
  632.2 2.0 fusion.24
  634.2 7.0 all-to-all-start
  641.2 0.7 mul.406
  641.9 40.8 %all-to-all-done = s16[16,64,1024]{2,1,0:T(8,128)(2,1)S(1)} async-done(((s16[16,64,1024]{2,1,0:T(8,128)(2,1)}), s16[16,64,1024]{2,1,0:T(8,128)(2,1)S(1)}, u32[]{:S(2)}, u32[]{:S(2)}) %all-to-all-start) | async-done | bytes 2097184 | tf_op jit(solution)/shard_map/all_to_all | solution.py:249
  682.7 10.9 %all-to-all-start.1 = ((f32[16,1,1024]{2,1,0:T(1,128)}), f32[16,1,1024]{2,1,0:T(1,128)S(1)}, u32[]{:S(2)}, u32[]{:S(2)}) async-start(f32[16,1,1024]{2,1,0:T(1,128)} %mul.406), calls=%async_computation.2 | async-start | bytes 131072 | tf_op jit(solution)/shard_map/all_to_all | solution.py:250
  693.6 0.7 convert_bitcast_fusion
  694.3 2.3 copy.6
  696.6 3.0 all-to-all-done.1
  699.6 4.5 broadcast_multiply_fusion
  (81 shorter events, 3.2 us)
Async XLA Ops:
  6.5 179.9 %reduce-scatter.2.cloned.1.call-start = ((), (), s32[]{:S(2)}) async-start(), calls=%async_computation.3 | async-start | bytes 4456448 | tf_op jit(solution)/shard_map/reduce_scatter | solution.py:226
  10.3 48.3 %collective-permute-start = (bf16[1024,1024]{1,0:T(8,128)(2,1)S(1)}, bf16[1024,1024]{1,0:T(8,128)(2,1)}, u32[]{:S(2)}, u32[]{:S(2)}) collective-permute-start(bf16[1024,1024]{1,0:T(8,128)(2,1)S(1)} %get-tuple-element.21), channel_id=1, source_target_pairs={{0,1},{2,3},{4,5},{6,7},{8,9},{10,11},{12,13},{14,15},{16,17},{18,... | collective-permute-start | bytes 6291464 | tf_op jit(solution)/shard_map/ppermute | solution.py:211
  18.1 79.6 %collective-permute-start.13 = (bf16[1024,2048]{1,0:T(8,128)(2,1)}, bf16[1024,2048]{1,0:T(8,128)(2,1)}, u32[]{:S(2)}, u32[]{:S(2)}) collective-permute-start(bf16[1024,2048]{1,0:T(8,128)(2,1)} %pad_maximum_fusion.3), channel_id=1, source_target_pairs={{0,2},{2,0},{4,6},{6,4},{8,10},{10,8},{12,14},{14,12},{16,18},{18,... | collective-permute-start | bytes 12582920 | tf_op jit(solution)/shard_map/ppermute | solution.py:189
  79.1 18.6 %collective-permute-start.1 = (bf16[1024,1024]{1,0:T(8,128)(2,1)S(1)}, bf16[1024,1024]{1,0:T(8,128)(2,1)}, u32[]{:S(2)}, u32[]{:S(2)}) collective-permute-start(bf16[1024,1024]{1,0:T(8,128)(2,1)S(1)} %get-tuple-element.6), channel_id=1, source_target_pairs={{0,2},{2,0},{4,6},{6,4},{8,10},{10,8},{12,14},{14,12},{16,18},{18,... | collective-permute-start | bytes 6291464 | tf_op jit(solution)/shard_map/ppermute | solution.py:189
  80.8 4.9 copy-start.3
  85.7 117.2 %collective-permute-start.2 = (bf16[1024,2048]{1,0:T(8,128)(2,1)}, bf16[1024,2048]{1,0:T(8,128)(2,1)}, u32[]{:S(2)}, u32[]{:S(2)}) collective-permute-start(bf16[1024,2048]{1,0:T(8,128)(2,1)} %pad_maximum_fusion), channel_id=1, source_target_pairs={{0,2},{2,0},{4,6},{6,4},{8,10},{10,8},{12,14},{14,12},{16,18},{18,... | collective-permute-start | bytes 12582920 | tf_op jit(solution)/shard_map/ppermute | solution.py:189
  88.2 26.8 %collective-permute-start.5 = (bf16[1024,2048]{1,0:T(8,128)(2,1)}, bf16[1024,2048]{1,0:T(8,128)(2,1)}, u32[]{:S(2)}, u32[]{:S(2)}) collective-permute-start(bf16[1024,2048]{1,0:T(8,128)(2,1)} %pad_maximum_fusion.1), channel_id=1, source_target_pairs={{0,2},{2,0},{4,6},{6,4},{8,10},{10,8},{12,14},{14,12},{16,18},{18,... | collective-permute-start | bytes 12582920 | tf_op jit(solution)/shard_map/ppermute | solution.py:189
  91.1 41.4 %collective-permute-start.10 = (bf16[1024,2048]{1,0:T(8,128)(2,1)}, bf16[1024,2048]{1,0:T(8,128)(2,1)}, u32[]{:S(2)}, u32[]{:S(2)}) collective-permute-start(bf16[1024,2048]{1,0:T(8,128)(2,1)} %pad_maximum_fusion.2), channel_id=1, source_target_pairs={{0,2},{2,0},{4,6},{6,4},{8,10},{10,8},{12,14},{14,12},{16,18},{18,... | collective-permute-start | bytes 12582920 | tf_op jit(solution)/shard_map/ppermute | solution.py:189
  97.2 337.4 %all-gather.2.cloned.1.call-start = ((), (), s32[]{:S(2)}) async-start(), calls=%async_computation.4 | async-start | bytes 4456448 | tf_op jit(solution)/shard_map/all_gather | solution.py:227
  97.7 7.2 %copy-start.10 = (bf16[1024,1024]{1,0:T(8,128)(2,1)S(1)}, bf16[1024,1024]{1,0:T(8,128)(2,1)}, u32[]{:S(2)}) copy-start(bf16[1024,1024]{1,0:T(8,128)(2,1)} %get-tuple-element.7) | copy-start | bytes 6291460
  97.7 7.2 %copy-start.11 = (bf16[1024,1024]{1,0:T(8,128)(2,1)S(1)}, bf16[1024,1024]{1,0:T(8,128)(2,1)}, u32[]{:S(2)}) copy-start(bf16[1024,1024]{1,0:T(8,128)(2,1)} %get-tuple-element.8) | copy-start | bytes 6291460
  109.5 4.0 copy-start.1
  113.6 80.4 %collective-permute-start.14 = (s16[1024,1024]{1,0:T(8,128)(2,1)}, s16[1024,1024]{1,0:T(8,128)(2,1)}, u32[]{:S(2)}, u32[]{:S(2)}) collective-permute-start(s16[1024,1024]{1,0:T(8,128)(2,1)} %fusion.30), channel_id=1, source_target_pairs={{0,4},{2,6},{4,0},{6,2},{8,12},{10,14},{12,8},{14,10},{16,20},{18,... | collective-permute-start | bytes 6291464 | tf_op jit(solution)/shard_map/ppermute | solution.py:189
  114.8 7.9 %copy-start.8 = (bf16[1024,1024]{1,0:T(8,128)(2,1)S(1)}, bf16[1024,1024]{1,0:T(8,128)(2,1)}, u32[]{:S(2)}) copy-start(bf16[1024,1024]{1,0:T(8,128)(2,1)} %get-tuple-element.15) | copy-start | bytes 6291460
  114.8 7.9 %copy-start.9 = (bf16[1024,1024]{1,0:T(8,128)(2,1)S(1)}, bf16[1024,1024]{1,0:T(8,128)(2,1)}, u32[]{:S(2)}) copy-start(bf16[1024,1024]{1,0:T(8,128)(2,1)} %get-tuple-element.16) | copy-start | bytes 6291460
  114.8 79.0 %collective-permute-start.15 = (f32[8,1024]{1,0:T(8,128)S(1)}, f32[8,1024]{1,0:T(8,128)S(1)}, u32[]{:S(2)}, u32[]{:S(2)}) collective-permute-start(f32[8,1024]{1,0:T(8,128)S(1)} %get-tuple-element.37), channel_id=1, source_target_pairs={{0,4},{2,6},{4,0},{6,2},{8,12},{10,14},{12,8},{14,10},{16,20},{18,... | collective-permute-start | bytes 98312 | tf_op jit(solution)/shard_map/ppermute | solution.py:189
  127.3 4.0 copy-start
  131.2 96.4 %collective-permute-start.6 = (s16[1024,1024]{1,0:T(8,128)(2,1)}, s16[1024,1024]{1,0:T(8,128)(2,1)}, u32[]{:S(2)}, u32[]{:S(2)}) collective-permute-start(s16[1024,1024]{1,0:T(8,128)(2,1)} %fusion.36), channel_id=1, source_target_pairs={{0,4},{2,6},{4,0},{6,2},{8,12},{10,14},{12,8},{14,10},{16,20},{18,... | collective-permute-start | bytes 6291464 | tf_op jit(solution)/shard_map/ppermute | solution.py:189
  132.5 7.4 %copy-start.6 = (bf16[1024,1024]{1,0:T(8,128)(2,1)S(1)}, bf16[1024,1024]{1,0:T(8,128)(2,1)}, u32[]{:S(2)}) copy-start(bf16[1024,1024]{1,0:T(8,128)(2,1)} %get-tuple-element.11) | copy-start | bytes 6291460
  132.5 7.4 %copy-start.7 = (bf16[1024,1024]{1,0:T(8,128)(2,1)S(1)}, bf16[1024,1024]{1,0:T(8,128)(2,1)}, u32[]{:S(2)}) copy-start(bf16[1024,1024]{1,0:T(8,128)(2,1)} %get-tuple-element.12) | copy-start | bytes 6291460
  132.5 94.6 %collective-permute-start.7 = (f32[8,1024]{1,0:T(8,128)S(1)}, f32[8,1024]{1,0:T(8,128)S(1)}, u32[]{:S(2)}, u32[]{:S(2)}) collective-permute-start(f32[8,1024]{1,0:T(8,128)S(1)} %get-tuple-element.29), channel_id=1, source_target_pairs={{0,4},{2,6},{4,0},{6,2},{8,12},{10,14},{12,8},{14,10},{16,20},{18,... | collective-permute-start | bytes 98312 | tf_op jit(solution)/shard_map/ppermute | solution.py:189
  186.5 11.5 %slice-start.4 = ((s8[8388608]{0:T(1024)(128)(4,1)}), s8[4194304]{0:T(1024)(128)(4,1)S(1)}, s32[]{:S(2)}) async-start(s8[8388608]{0:T(1024)(128)(4,1)} %bitcast.136), calls=%async_computation.9 | async-start | bytes 8388608
  189.3 8.6 %slice-start.5 = ((s8[8388608]{0:T(1024)(128)(4,1)}), s8[4194304]{0:T(1024)(128)(4,1)S(1)}, s32[]{:S(2)}) async-start(s8[8388608]{0:T(1024)(128)(4,1)} %bitcast.136), calls=%async_computation.10 | async-start | bytes 8388608
  193.7 133.1 %collective-permute-start.11 = (s16[1024,1024]{1,0:T(8,128)(2,1)}, s16[1024,1024]{1,0:T(8,128)(2,1)}, u32[]{:S(2)}, u32[]{:S(2)}) collective-permute-start(s16[1024,1024]{1,0:T(8,128)(2,1)} %fusion.32), channel_id=1, source_target_pairs={{0,4},{2,6},{4,0},{6,2},{8,12},{10,14},{12,8},{14,10},{16,20},{18,... | collective-permute-start | bytes 6291464 | tf_op jit(solution)/shard_map/ppermute | solution.py:189
  202.4 11.5 %copy-start.4 = (bf16[1024,1024]{1,0:T(8,128)(2,1)S(1)}, bf16[1024,1024]{1,0:T(8,128)(2,1)}, u32[]{:S(2)}) copy-start(bf16[1024,1024]{1,0:T(8,128)(2,1)} %get-tuple-element.5) | copy-start | bytes 6291460
  202.4 11.5 %copy-start.5 = (bf16[1024,1024]{1,0:T(8,128)(2,1)S(1)}, bf16[1024,1024]{1,0:T(8,128)(2,1)}, u32[]{:S(2)}) copy-start(bf16[1024,1024]{1,0:T(8,128)(2,1)} %get-tuple-element.19) | copy-start | bytes 6291460
  202.4 124.5 %collective-permute-start.16 = (s16[1024,1024]{1,0:T(8,128)(2,1)}, s16[1024,1024]{1,0:T(8,128)(2,1)}, u32[]{:S(2)}, u32[]{:S(2)}) collective-permute-start(s16[1024,1024]{1,0:T(8,128)(2,1)} %fusion.28), channel_id=1, source_target_pairs={{0,8},{2,10},{4,12},{6,14},{8,0},{10,2},{12,4},{14,6},{16,24},{18,... | collective-permute-start | bytes 6291464 | tf_op jit(solution)/shard_map/ppermute | solution.py:189
  202.9 25.8 %slice-start.2 = ((s8[8388608]{0:T(1024)(128)(4,1)}), s8[4194304]{0:T(1024)(128)(4,1)S(1)}, s32[]{:S(2)}) async-start(s8[8388608]{0:T(1024)(128)(4,1)} %bitcast.134), calls=%async_computation.7 | async-start | bytes 8388608
  213.8 14.9 %slice-start.3 = ((s8[8388608]{0:T(1024)(128)(4,1)}), s8[4194304]{0:T(1024)(128)(4,1)S(1)}, s32[]{:S(2)}) async-start(s8[8388608]{0:T(1024)(128)(4,1)} %bitcast.134), calls=%async_computation.8 | async-start | bytes 8388608
  221.9 4.0 copy-start.2
  222.4 104.4 %slice-start = ((s8[8388608]{0:T(1024)(128)(4,1)}), s8[4194304]{0:T(1024)(128)(4,1)S(1)}, s32[]{:S(2)}) async-start(s8[8388608]{0:T(1024)(128)(4,1)} %bitcast.132), calls=%async_computation.5 | async-start | bytes 8388608
  225.9 116.6 %collective-permute-start.3 = (s16[1024,1024]{1,0:T(8,128)(2,1)S(1)}, s16[1024,1024]{1,0:T(8,128)(2,1)}, u32[]{:S(2)}, u32[]{:S(2)}) collective-permute-start(s16[1024,1024]{1,0:T(8,128)(2,1)S(1)} %fusion.38), channel_id=1, source_target_pairs={{0,4},{2,6},{4,0},{6,2},{8,12},{10,14},{12,8},{14,10},{16,20},{18,... | collective-permute-start | bytes 6291464 | tf_op jit(solution)/shard_map/ppermute | solution.py:189
  227.1 98.6 %collective-permute-start.12 = (f32[8,1024]{1,0:T(8,128)S(1)}, f32[8,1024]{1,0:T(8,128)S(1)}, u32[]{:S(2)}, u32[]{:S(2)}) collective-permute-start(f32[8,1024]{1,0:T(8,128)S(1)} %get-tuple-element.34), channel_id=1, source_target_pairs={{0,4},{2,6},{4,0},{6,2},{8,12},{10,14},{12,8},{14,10},{16,20},{18,... | collective-permute-start | bytes 98312 | tf_op jit(solution)/shard_map/ppermute | solution.py:189
  227.7 99.2 %slice-start.1 = ((s8[8388608]{0:T(1024)(128)(4,1)}), s8[4194304]{0:T(1024)(128)(4,1)S(1)}, s32[]{:S(2)}) async-start(s8[8388608]{0:T(1024)(128)(4,1)} %bitcast.132), calls=%async_computation.6 | async-start | bytes 8388608
  227.7 99.2 %collective-permute-start.17 = (f32[8,1024]{1,0:T(8,128)S(1)}, f32[8,1024]{1,0:T(8,128)S(1)}, u32[]{:S(2)}, u32[]{:S(2)}) collective-permute-start(f32[8,1024]{1,0:T(8,128)S(1)} %get-tuple-element.36), channel_id=1, source_target_pairs={{0,8},{2,10},{4,12},{6,14},{8,0},{10,2},{12,4},{14,6},{16,24},{18,... | collective-permute-start | bytes 98312 | tf_op jit(solution)/shard_map/ppermute | solution.py:189
  325.6 90.8 %collective-permute-start.8 = (s16[1024,1024]{1,0:T(8,128)(2,1)}, s16[1024,1024]{1,0:T(8,128)(2,1)}, u32[]{:S(2)}, u32[]{:S(2)}) collective-permute-start(s16[1024,1024]{1,0:T(8,128)(2,1)} %fusion.34), channel_id=1, source_target_pairs={{0,8},{2,10},{4,12},{6,14},{8,0},{10,2},{12,4},{14,6},{16,24},{18,... | collective-permute-start | bytes 6291464 | tf_op jit(solution)/shard_map/ppermute | solution.py:189
  337.0 93.3 %collective-permute-start.18 = (s16[1024,1024]{1,0:T(8,128)(2,1)}, s16[1024,1024]{1,0:T(8,128)(2,1)}, u32[]{:S(2)}, u32[]{:S(2)}) collective-permute-start(s16[1024,1024]{1,0:T(8,128)(2,1)} %fusion.26), channel_id=1, source_target_pairs={{0,16},{2,18},{4,20},{6,22},{8,24},{10,26},{12,28},{14,30},{16,0},... | collective-permute-start | bytes 6291464 | tf_op jit(solution)/shard_map/ppermute | solution.py:189
  339.3 3.2 collective-permute-start.4
  340.6 75.8 %collective-permute-start.9 = (f32[8,1024]{1,0:T(8,128)S(1)}, f32[8,1024]{1,0:T(8,128)S(1)}, u32[]{:S(2)}, u32[]{:S(2)}) collective-permute-start(f32[8,1024]{1,0:T(8,128)S(1)} %get-tuple-element.27), channel_id=1, source_target_pairs={{0,8},{2,10},{4,12},{6,14},{8,0},{10,2},{12,4},{14,6},{16,24},{18,... | collective-permute-start | bytes 98312 | tf_op jit(solution)/shard_map/ppermute | solution.py:189
  342.5 87.7 %collective-permute-start.19 = (f32[8,1024]{1,0:T(8,128)S(1)}, f32[8,1024]{1,0:T(8,128)S(1)}, u32[]{:S(2)}, u32[]{:S(2)}) collective-permute-start(f32[8,1024]{1,0:T(8,128)S(1)} %get-tuple-element.31), channel_id=1, source_target_pairs={{0,16},{2,18},{4,20},{6,22},{8,24},{10,26},{12,28},{14,30},{16,0},... | collective-permute-start | bytes 98312 | tf_op jit(solution)/shard_map/ppermute | solution.py:189
  420.7 13.9 %copy-start.12 = (f32[1024]{0:T(1024)S(1)}, f32[1024]{0:T(1024)}, u32[]{:S(2)}) copy-start(f32[1024]{0:T(1024)} %param.5) | copy-start | bytes 12292
  434.6 178.0 %slice-start.6 = ((s8[8388608]{0:T(1024)(128)(4,1)}), s8[4194304]{0:T(1024)(128)(4,1)S(1)}, s32[]{:S(2)}) async-start(s8[8388608]{0:T(1024)(128)(4,1)} %bitcast.138), calls=%async_computation.11 | async-start | bytes 8388608
  437.5 175.1 %slice-start.7 = ((s8[8388608]{0:T(1024)(128)(4,1)}), s8[4194304]{0:T(1024)(128)(4,1)S(1)}, s32[]{:S(2)}) async-start(s8[8388608]{0:T(1024)(128)(4,1)} %bitcast.138), calls=%async_computation.12 | async-start | bytes 8388608
  634.2 48.5 %all-to-all-start = ((s16[16,64,1024]{2,1,0:T(8,128)(2,1)}), s16[16,64,1024]{2,1,0:T(8,128)(2,1)S(1)}, u32[]{:S(2)}, u32[]{:S(2)}) async-start(s16[16,64,1024]{2,1,0:T(8,128)(2,1)} %bitcast.141), calls=%async_computation.1 | async-start | bytes 4194304 | tf_op jit(solution)/shard_map/all_to_all | solution.py:249
  682.7 16.9 %all-to-all-start.1 = ((f32[16,1,1024]{2,1,0:T(1,128)}), f32[16,1,1024]{2,1,0:T(1,128)S(1)}, u32[]{:S(2)}, u32[]{:S(2)}) async-start(f32[16,1,1024]{2,1,0:T(1,128)} %mul.406), calls=%async_computation.2 | async-start | bytes 131072 | tf_op jit(solution)/shard_map/all_to_all | solution.py:250
Sparse Core Ops, SparseCore 0:
  97.3 89.0 reduce-scatter.1
  188.8 69.1 all-gather.1
